TPU v7x, 32 devices: a whole 2x2x4 slice. The times are simulated.
32 devices in a mesh: sec: 2 (over x), gx: 4 (over y, core), gy: 4 (over z).
Axes of the slice: x: 2, y: 2, z: 4, core: 2. Of those that a mesh axis runs over, the one named last changes fastest.
Arguments:
- pressure: float32 [50, 128, 512], P(None, ('sec', 'gx'), 'gy'), may hold values from -4 to 4
- pressure_old: float32 [50, 128, 512], P(None, ('sec', 'gx'), 'gy'), may hold values from -4 to 4
- conductivity: float32 [50, 128, 512], P(None, ('sec', 'gx'), 'gy'), may hold values from 0.3 to 3
- vg_alpha: float32 [50, 128, 512], P(None, ('sec', 'gx'), 'gy'), may hold values from 0.5 to 4
- porosity: float32 [50, 128, 512], P(None, ('sec', 'gx'), 'gy'), may hold values from 0.3 to 0.5
- land_mask: int32 [128, 512], P(('sec', 'gx'), 'gy'), may hold values 0 or 1
- nitrate: float32 [10, 8192], P(None, ('sec', 'gx', 'gy')), may hold values from 0.5 to 2
- patch_column: int32 [8192], P(('sec', 'gx', 'gy')), may hold values from 0 to 2047
- crop_type: int32 [8192], P(('sec', 'gx', 'gy')), may hold values from 0 to 7
- patch_weight: float32 [8192], P(('sec', 'gx', 'gy')), may hold values from 0.2 to 2
- rain: float32 [8192], P(('sec', 'gx', 'gy')), may hold values from 0.1 to 1
- root_decay: float32 [8], replicated, may hold values from 0.05 to 0.8
Outputs:
- residual: float32 [50, 128, 512], P(None, ('sec', 'gx'), 'gy')
- nitrate_out: float32 [10, 8192], P(None, ('sec', 'gx', 'gy'))
All inputs are finite; a program needn't handle non-finite values. No bound on the sum of `land_mask` on one device may be relied on, other than what follows from the above.
Results may differ from a plain program's by a relative error of at most 0.0003.
The roundings to bfloat16 on the way count: a program that leaves them out, or rounds other values in their place, can miss the bound.
Values may be sent and summed in bfloat16 or wider, within the bound.
No kernel may reach another device: no remote copies, remote signals or barrier semaphores. Data moves between devices by JAX's collectives and lax.ppermute only.
A program may use at most 192 MiB of HBM per device.

v0:
```python
import jax
import jax.numpy as jnp
from jax import lax
from jax.sharding import PartitionSpec as P

NSUB = 4


def with_halo(value, sides, width):
    for axis, dim in sides:
        peers, length = (lax.axis_size(axis), value.shape[dim])
        up = [(i, (i + 1) % peers) for i in range(peers - 1)]
        down = [(j, i) for i, j in up]
        last = lax.slice_in_dim(value, length - width, length, axis=dim)
        leading = lax.slice_in_dim(value, 0, width, axis=dim)
        before = lax.ppermute(last, axis, up)
        after = lax.ppermute(leading, axis, down)
        value = jnp.concatenate([before, value, after], axis=dim)
    return value


def saturation(head, alpha_field):
    suction = jax.nn.softplus(-head)
    scaled = alpha_field * suction
    return 1.0 / jnp.sqrt(1.0 + scaled * scaled)


def outflow(pressure, conduct, head_pad, cond_pad):
    head_x = head_pad[:, :, 1:-1]
    cond_x = cond_pad[:, :, 1:-1]
    flux_x = 0.5 * (cond_x[:, :-1] + cond_x[:, 1:]) * (head_x[:, :-1] - head_x[:, 1:])
    head_y = head_pad[:, 1:-1, :]
    cond_y = cond_pad[:, 1:-1, :]
    flux_y = 0.5 * (cond_y[:, :, :-1] + cond_y[:, :, 1:]) * (head_y[:, :, :-1] - head_y[:, :, 1:])
    flux_z = 0.5 * (conduct[:-1] + conduct[1:]) * (pressure[:-1] - pressure[1:] + 1.0)
    zero_top = jnp.zeros_like(conduct[:1])
    flux_z = jnp.concatenate([zero_top, flux_z, conduct[-1:]], 0)
    return (
        flux_x[:, 1:]
        - flux_x[:, :-1]
        + (flux_y[:, :, 1:] - flux_y[:, :, :-1])
        + (flux_z[1:] - flux_z[:-1])
    )


def deposit(values, targets, columns):
    slots = targets.shape[0]
    stride = 512 if slots % 512 == 0 else slots
    cells = jnp.arange(columns, dtype=jnp.int32)
    total = jnp.zeros((values.shape[0], columns), jnp.float32)
    for start in range(0, slots, stride):
        onehot = (targets[start : start + stride, None] == cells[None, :]).astype(jnp.float32)
        total = total + jnp.dot(
            values[:, start : start + stride],
            onehot,
            precision=lax.Precision.HIGHEST,
            preferred_element_type=jnp.float32,
        )
    return total


def patch_sources(sat_p, kinds_of, root_decay, weights, rainfall, top):
    kinds = jnp.arange(root_decay.shape[0], dtype=jnp.int32)
    decay = jnp.sum(
        jnp.where(kinds_of[None, :] == kinds[:, None], root_decay[:, None], 0.0), axis=0
    )
    levels = jnp.arange(top, dtype=jnp.float32) + 0.5
    profile = jnp.exp(-levels[:, None] * decay[None, :])
    profile = profile / jnp.sum(profile, axis=0, keepdims=True)
    extraction = weights[None, :] * profile * sat_p
    inflow = rainfall * (1.0 - sat_p[0])
    return jnp.concatenate([(inflow - extraction[0])[None], -extraction[1:]], 0)


def per_device(
    pressure,
    pressure_old,
    conductivity,
    vg_alpha,
    porosity,
    land_mask,
    nitrate,
    patch_column,
    crop_type,
    patch_weight,
    rain,
    root_decay,
):
    layers, width_x, width_y = pressure.shape
    top = nitrate.shape[0]
    kind_count = root_decay.shape[0]
    columns = width_x * width_y
    slots = patch_column.shape[0]
    owners = lax.axis_size(("gx", "gy"))
    per_block = slots // owners
    wet = saturation(pressure, vg_alpha)
    wet_old = saturation(pressure_old, vg_alpha)
    conduct = conductivity * wet * wet * wet
    sat_top = wet[:top].reshape(top, columns).astype(jnp.bfloat16)
    coded = patch_column * kind_count + crop_type
    codes_in = lax.all_to_all(
        coded.reshape(1, slots), ("gx", "gy"), split_axis=1, concat_axis=1, tiled=True
    )[0]
    ids_in = codes_in // kind_count
    whole = lax.all_gather(sat_top, ("gx", "gy"), axis=1, tiled=True)
    offsets = jnp.arange(slots, dtype=jnp.int32) // per_block * columns
    patch_sat = jnp.take(whole, offsets + patch_column, axis=1)
    sat_p = patch_sat.astype(jnp.float32)
    sources = patch_sources(sat_p, crop_type, root_decay, patch_weight, rain, top)
    received = lax.all_to_all(
        sources.astype(jnp.bfloat16), ("gx", "gy"), split_axis=1, concat_axis=1, tiled=True
    ).astype(sources.dtype)
    nitrogen = nitrate
    for step in range(NSUB):
        upper = jnp.concatenate([nitrogen[:1], nitrogen[:-1]], 0)
        lower = jnp.concatenate([nitrogen[1:], nitrogen[-1:]], 0)
        nitrogen = (
            nitrogen + 0.2 * (upper + lower - 2.0 * nitrogen) - 0.3 * sat_p * sat_p * nitrogen
        )
    stacked = jnp.stack([pressure, conduct])
    padded = with_halo(stacked, ((("sec", "gx"), 2), ("gy", 3)), 1)
    residual = porosity * (wet - wet_old) + outflow(pressure, conduct, padded[0], padded[1])
    column_source = deposit(received, ids_in, columns).reshape(top, width_x, width_y)
    column_source = column_source * land_mask.astype(jnp.float32)[None]
    residual = jnp.concatenate([residual[:top] - column_source, residual[top:]], 0)
    return (residual, nitrogen)


def solution(mesh):
    placed = (
        P(None, ("sec", "gx"), "gy"),
        P(None, ("sec", "gx"), "gy"),
        P(None, ("sec", "gx"), "gy"),
        P(None, ("sec", "gx"), "gy"),
        P(None, ("sec", "gx"), "gy"),
        P(("sec", "gx"), "gy"),
        P(None, ("sec", "gx", "gy")),
        P(("sec", "gx", "gy")),
        P(("sec", "gx", "gy")),
        P(("sec", "gx", "gy")),
        P(("sec", "gx", "gy")),
        P(),
    )
    return jax.shard_map(
        per_device,
        mesh=mesh,
        in_specs=placed,
        out_specs=(P(None, ("sec", "gx"), "gy"), P(None, ("sec", "gx", "gy"))),
        check_vma=False,
    )
```

profile of v0, /device:TPU:0, one launch (start us, length us, event | category | flops | bytes accessed | tf_op | source)
XLA Modules:
  0.0 239.4 jit_solution(622747574008032368)
XLA Ops:
  0.7 1.8 multiply_multiply_fusion
  2.5 1.3 collective-permute-start.1
  3.8 3.0 %collective-permute-start = (f32[2,50,1,128]{3,1,2,0:T(8,128)S(1)}, f32[2,50,1,128]{3,1,2,0:T(8,128)S(1)}, u32[]{:S(2)}, u32[]{:S(2)}) collective-permute-start(f32[2,50,1,128]{3,1,2,0:T(8,128)S(1)} %get-tuple-element.22), channel_id=1, source_target_pairs={{0,4},{4,8},{8,12},{12,16},{16,20},{20,24},{24,28},{1,5},{5,9},{9,... | collective-permute-start | bytes 153608 | tf_op jit(solution)/shard_map/ppermute | solution.py:16
  6.9 0.7 all_to_all.14
  7.6 9.0 %all-to-all-start.1 = ((s32[1,16,16]{2,0,1:T(1,128)}), s32[1,16,16]{2,0,1:T(1,128)S(1)}, u32[]{:S(2)}, u32[]{:S(2)}) async-start(s32[1,16,16]{2,0,1:T(1,128)} %all_to_all.14), calls=%async_computation.1 | async-start | bytes 16384 | tf_op jit(solution)/shard_map/all_to_all | solution.py:101
  16.9 190.1 %all_gather.3 = bf16[10,32768]{0,1:T(8,128)(2,1)} all-gather(bf16[10,2048]{0,1:T(8,128)(2,1)S(1)} %bitcast.27), channel_id=1, replica_groups=mesh['sec'=2,'gx'=4,'gy'=4] {'gx','gy'}, dimensions={1}, use_global_device_ids=true | all-gather | bytes 696320 | tf_op jit(solution)/shard_map/all_gather | solution.py:105
  207.0 5.2 %gather_fusion = bf16[256,10]{1,0:T(8,128)(2,1)S(1)} fusion(bf16[10,32768]{0,1:T(8,128)(2,1)} %all_gather.3, s32[1024]{0:T(1024)S(1)} %pad_clamp_fusion), kind=kCustom, calls=%fused_computation | custom fusion | bytes 11264 | tf_op jit(solution)/shard_map/jit(_take)/gather | solution.py:107
  212.7 0.6 fusion.46
  213.4 0.9 fusion.26
  214.5 0.7 pad_maximum_fusion.3
  215.2 0.6 multiply_add_fusion
  215.8 0.6 slice.219
  216.4 0.6 convert_element_type.16
  217.0 3.5 %all-to-all-start = ((bf16[10,16,16]{2,0,1:T(8,128)(2,1)}), bf16[10,16,16]{2,0,1:T(8,128)(2,1)S(1)}, u32[]{:S(2)}, u32[]{:S(2)}) async-start(bf16[10,16,16]{2,0,1:T(8,128)(2,1)} %pad_maximum_fusion.3), calls=%async_computation | async-start | bytes 131072 | tf_op jit(solution)/shard_map/all_to_all | solution.py:110
  220.5 0.5 broadcast.146
  221.0 0.6 reduce.3
  221.7 0.6 copy-done.4
  222.3 0.6 copy-done.6
  223.3 1.0 copy.195
  224.4 1.3 collective-permute-start.3
  225.6 0.4 copy.194
  226.1 5.1 %collective-permute-start.2 = (f32[2,50,18,1]{1,0,3,2:T(2,128)S(1)}, f32[2,50,18,1]{1,0,3,2:T(2,128)}, u32[]{:S(2)}, u32[]{:S(2)}) collective-permute-start(f32[2,50,18,1]{1,0,3,2:T(2,128)S(1)} %copy.194), channel_id=1, source_target_pairs={{0,1},{1,2},{2,3},{4,5},{5,6},{6,7},{8,9},{9,10},{10,11},{12,13},{... | collective-permute-start | bytes 21608 | tf_op jit(solution)/shard_map/ppermute | solution.py:16
  231.2 0.6 and_select_fusion
  231.9 0.7 reshape.92
  232.6 0.5 copy.197
  233.0 1.2 copy.196
  234.3 0.9 pad_maximum_fusion
  235.3 0.5 fusion.10
  235.9 0.6 fusion.12
  237.3 0.7 fusion.24
  238.1 0.5 fusion.5
  238.6 0.8 copy.206
  (80 shorter events, 2.5 us)
Async XLA Ops:
  0.6 6.2 %copy-start.14 = (s32[256]{0:T(256)S(1)}, s32[256]{0:T(256)}, u32[]{:S(2)}) copy-start(s32[256]{0:T(256)} %param.19) | copy-start | bytes 3076
  0.6 6.2 %copy-start.15 = (s32[256]{0:T(256)S(1)}, s32[256]{0:T(256)}, u32[]{:S(2)}) copy-start(s32[256]{0:T(256)} %param.20) | copy-start | bytes 3076
  0.7 15.9 %copy-start.8 = (f32[10,256]{1,0:T(8,128)S(1)}, f32[10,256]{1,0:T(8,128)}, u32[]{:S(2)}) copy-start(f32[10,256]{1,0:T(8,128)} %param.18) | copy-start | bytes 30724
  2.5 219.2 %collective-permute-start.1 = (f32[2,50,1,128]{3,1,2,0:T(8,128)S(1)}, f32[2,50,1,128]{3,1,2,0:T(8,128)S(1)}, u32[]{:S(2)}, u32[]{:S(2)}) collective-permute-start(f32[2,50,1,128]{3,1,2,0:T(8,128)S(1)} %get-tuple-element.23), channel_id=1, source_target_pairs={{4,0},{8,4},{12,8},{16,12},{20,16},{24,20},{28,24},{5,1},{9,5},{13... | collective-permute-start | bytes 153608 | tf_op jit(solution)/shard_map/ppermute | solution.py:17
  3.8 217.9 %collective-permute-start = (f32[2,50,1,128]{3,1,2,0:T(8,128)S(1)}, f32[2,50,1,128]{3,1,2,0:T(8,128)S(1)}, u32[]{:S(2)}, u32[]{:S(2)}) collective-permute-start(f32[2,50,1,128]{3,1,2,0:T(8,128)S(1)} %get-tuple-element.22), channel_id=1, source_target_pairs={{0,4},{4,8},{8,12},{12,16},{16,20},{20,24},{24,28},{1,5},{5,9},{9,... | collective-permute-start | bytes 153608 | tf_op jit(solution)/shard_map/ppermute | solution.py:16
  7.6 209.4 %all-to-all-start.1 = ((s32[1,16,16]{2,0,1:T(1,128)}), s32[1,16,16]{2,0,1:T(1,128)S(1)}, u32[]{:S(2)}, u32[]{:S(2)}) async-start(s32[1,16,16]{2,0,1:T(1,128)} %all_to_all.14), calls=%async_computation.1 | async-start | bytes 16384 | tf_op jit(solution)/shard_map/all_to_all | solution.py:101
  16.9 195.6 %copy-start.19 = (f32[8]{0:T(128)S(1)}, f32[8]{0:T(128)}, u32[]{:S(2)}) copy-start(f32[8]{0:T(128)} %param.23) | copy-start | bytes 100
  16.9 195.8 %copy-start.16 = (f32[256]{0:T(256)S(1)}, f32[256]{0:T(256)}, u32[]{:S(2)}) copy-start(f32[256]{0:T(256)} %param.21) | copy-start | bytes 3076
  207.0 7.4 %copy-start.17 = (f32[256]{0:T(256)S(1)}, f32[256]{0:T(256)}, u32[]{:S(2)}) copy-start(f32[256]{0:T(256)} %param.22) | copy-start | bytes 3076
  207.0 9.4 %copy-start.10 = (s32[16,128]{1,0:T(8,128)S(1)}, s32[16,128]{1,0:T(8,128)}, u32[]{:S(2)}) copy-start(s32[16,128]{1,0:T(8,128)} %param.17) | copy-start | bytes 24580
  217.0 14.8 %all-to-all-start = ((bf16[10,16,16]{2,0,1:T(8,128)(2,1)}), bf16[10,16,16]{2,0,1:T(8,128)(2,1)S(1)}, u32[]{:S(2)}, u32[]{:S(2)}) async-start(bf16[10,16,16]{2,0,1:T(8,128)(2,1)} %pad_maximum_fusion.3), calls=%async_computation | async-start | bytes 131072 | tf_op jit(solution)/shard_map/all_to_all | solution.py:110
  221.7 0.6 copy-start.4
  222.3 0.6 copy-start.6
  224.4 8.2 %collective-permute-start.3 = (f32[2,50,18,1]{1,0,3,2:T(2,128)}, f32[2,50,18,1]{1,0,3,2:T(2,128)S(1)}, u32[]{:S(2)}, u32[]{:S(2)}) collective-permute-start(f32[2,50,18,1]{1,0,3,2:T(2,128)} %copy.195), channel_id=1, source_target_pairs={{1,0},{2,1},{3,2},{5,4},{6,5},{7,6},{9,8},{10,9},{11,10},{13,12},{... | collective-permute-start | bytes 21608 | tf_op jit(solution)/shard_map/ppermute | solution.py:17
  226.1 7.0 %collective-permute-start.2 = (f32[2,50,18,1]{1,0,3,2:T(2,128)S(1)}, f32[2,50,18,1]{1,0,3,2:T(2,128)}, u32[]{:S(2)}, u32[]{:S(2)}) collective-permute-start(f32[2,50,18,1]{1,0,3,2:T(2,128)S(1)} %copy.194), channel_id=1, source_target_pairs={{0,1},{1,2},{2,3},{4,5},{5,6},{6,7},{8,9},{9,10},{10,11},{12,13},{... | collective-permute-start | bytes 21608 | tf_op jit(solution)/shard_map/ppermute | solution.py:16
  231.8 2.4 %copy-start.5 = (f32[2,50,1,128]{3,1,2,0:T(8,128)S(1)}, f32[2,50,1,128]{3,1,2,0:T(8,128)}, u32[]{:S(2)}) copy-start(f32[2,50,1,128]{3,1,2,0:T(8,128)} %copy-done.4) | copy-start | bytes 153604
  231.8 2.4 %copy-start.7 = (f32[2,50,1,128]{3,1,2,0:T(8,128)S(1)}, f32[2,50,1,128]{3,1,2,0:T(8,128)}, u32[]{:S(2)}) copy-start(f32[2,50,1,128]{3,1,2,0:T(8,128)} %copy-done.6) | copy-start | bytes 153604
  235.8 1.0 copy-start
  235.8 1.1 copy-start.1
  235.9 1.2 copy-start.2
  235.9 1.4 copy-start.3
  235.9 1.4 copy-start.9
  237.2 0.8 copy-start.11
  237.2 0.8 copy-start.12
  237.2 0.8 copy-start.13
  237.2 0.8 copy-start.18
where the time goes:
time: 240 us; the launch traced here: 239 us
  blocking collectives  190 us (79%)
  starting transfers between devices  23.2 us (10%)
  local copies, waits for them, and re-layouts  15 us (6%)
  other arithmetic  9.55 us (4%)
    all_gather x1, blocking collectives, per_device(): whole = lax.all_gather(sat_top, ('gx', 'gy'), axis=1, tiled=True)  190 us
    all_to_all x1, starting transfers between devices, per_device(): lax.all_to_all(coded.reshape(1, slots), ('gx', 'gy'), split_axis=1, conca...  8.96 us
    ppermute x2, starting transfers between devices, with_halo(): before = lax.ppermute(last, axis, up)  8.17 us
    gather x2, local copies, waits for them, and re-layouts, per_device(): patch_sat = jnp.take(whole, offsets + patch_column, axis=1)  5.29 us
  transfers between devices with their start and end apart: 6, of which 0 were waited for; matrix products, arithmetic and copies ran while one was open for 6% of the time, Pallas kernels for 0%

commit v1 on v0

--- a/solution.py
+++ b/solution.py
@@ -4,6 +4,12 @@
 from jax.sharding import PartitionSpec as P
 
 NSUB = 4
+
+
+def in_order(tiles, dim):
+    shape = list(tiles.shape[1:])
+    shape[dim] *= tiles.shape[0]
+    return jnp.moveaxis(tiles, 0, dim).reshape(shape)
 
 
 def with_halo(value, sides, width):
@@ -102,7 +108,19 @@
         coded.reshape(1, slots), ("gx", "gy"), split_axis=1, concat_axis=1, tiled=True
     )[0]
     ids_in = codes_in // kind_count
-    whole = lax.all_gather(sat_top, ("gx", "gy"), axis=1, tiled=True)
+    size = lax.axis_size(("gx", "gy"))
+    pairs = [(i_2, (i_2 + 1) % size) for i_2 in range(size)]
+    back = [(b, a) for a, b in pairs]
+    lower_2, upper_2 = ([], [])
+    for step_2 in range(size - 1):
+        if step_2 % 2 == 0:
+            lower_2.append(lax.ppermute(lower_2[-1] if lower_2 else sat_top, ("gx", "gy"), pairs))
+        else:
+            upper_2.append(lax.ppermute(upper_2[-1] if upper_2 else sat_top, ("gx", "gy"), back))
+    blocks = jnp.stack([*lower_2[::-1], sat_top, *upper_2])
+    shift = lax.axis_index(("gx", "gy")) - len(lower_2)
+    blocks = blocks[(jnp.arange(size) - shift) % size]
+    whole = in_order(blocks, 1)
     offsets = jnp.arange(slots, dtype=jnp.int32) // per_block * columns
     patch_sat = jnp.take(whole, offsets + patch_column, axis=1)
     sat_p = patch_sat.astype(jnp.float32)

time: 240 us -> 110 us (0.46)
  blocking collectives: 190 us -> 0 us
  starting transfers between devices: 23.2 us -> 51.9 us
  waiting for transfers between devices: 0.02 us -> 13.7 us
  other arithmetic: 9.55 us -> 18.4 us
  local copies, waits for them, and re-layouts: 15 us -> 23.5 us
    all_gather x1 -> x0, blocking collectives: 190 us -> none  [per_device(): whole = lax.all_gather(sat_top, ('gx', 'gy'), axis=1, tiled=True)]
    ppermute x0 -> x15, starting transfers between devices: none -> 32.6 us  [the longest x7 28 us: per_device(): lax.ppermute(upper_2[-1] if upper_2 else sat_top, ('gx', 'gy'), back)]
    ppermute x0 -> x15, waiting for transfers between devices: none -> 8.31 us  [the longest x8 5.07 us: per_device(): lax.ppermute(lower_2[-1] if lower_2 else sat_top, ('gx', 'gy'), pairs)]
    reshape x0 -> x1, local copies, waits for them, and re-layouts: none -> 6.17 us  [in_order(): return jnp.moveaxis(tiles, 0, dim).reshape(shape)]
    all_to_all x1, waiting for transfers between devices: 0.01 us -> 4.88 us  [per_device(): lax.all_to_all(sources.astype(jnp.bfloat16), ('gx', 'gy'), split_axis=1,...]
    all_to_all x1, starting transfers between devices: 8.96 us -> 4.91 us  [per_device(): lax.all_to_all(coded.reshape(1, slots), ('gx', 'gy'), split_axis=1, conca...]
    sub x4, other arithmetic: 0.71 us -> 3.5 us  [per_device(): nitrogen + 0.2 * (upper + lower - 2.0 * nitrogen)]
  transfers between devices with their start and end apart: 6 -> 21, of which waited for: 0 -> 11; matrix products, arithmetic and copies ran while one was open for 6% -> 18% of each run, Pallas kernels for 0% -> 0%
where the time goes in v1:
time: 110 us; the launch traced here: 109 us
  starting transfers between devices  51.9 us (47%)
  local copies, waits for them, and re-layouts  23.5 us (21%)
  other arithmetic  18.4 us (17%)
  waiting for transfers between devices  13.7 us (12%)
  between operations  1.16 us (1%)
    ppermute x7, starting transfers between devices, per_device(): lax.ppermute(upper_2[-1] if upper_2 else sat_top, ('gx', 'gy'), back)  28 us
    ppermute x2, starting transfers between devices, with_halo(): before = lax.ppermute(last, axis, up)  8.18 us
    reshape x1, local copies, waits for them, and re-layouts, in_order(): return jnp.moveaxis(tiles, 0, dim).reshape(shape)  6.17 us
    gather x2, local copies, waits for them, and re-layouts, per_device(): patch_sat = jnp.take(whole, offsets + patch_column, axis=1)  5.48 us
    ppermute x8, waiting for transfers between devices, per_device(): lax.ppermute(lower_2[-1] if lower_2 else sat_top, ('gx', 'gy'), pairs)  5.07 us
    all_to_all x1, starting transfers between devices, per_device(): lax.all_to_all(coded.reshape(1, slots), ('gx', 'gy'), split_axis=1, conca...  4.91 us
    all_to_all x1, waiting for transfers between devices, per_device(): lax.all_to_all(sources.astype(jnp.bfloat16), ('gx', 'gy'), split_axis=1,...  4.88 us
    ppermute x8, starting transfers between devices, per_device(): lax.ppermute(lower_2[-1] if lower_2 else sat_top, ('gx', 'gy'), pairs)  4.66 us
  transfers between devices with their start and end apart: 21, of which 11 were waited for; matrix products, arithmetic and copies ran while one was open for 18% of the time, Pallas kernels for 0%

profile of v1, /device:TPU:0, one launch (start us, length us, event | category | flops | bytes accessed | tf_op | source)
XLA Modules:
  0.0 109.1 jit_solution(5815506025183570456)
XLA Ops:
  0.7 1.6 %multiply_multiply_fusion = (f32[50,16,128]{2,1,0:T(8,128)S(1)}, f32[50,16,128]{2,1,0:T(8,128)S(1)}) fusion(f32[50,16,128]{2,1,0:T(8,128)} %param.14, f32[50,16,128]{2,1,0:T(8,128)} %param.15, f32[50,16,128]{2,1,0:T(8,128)} %param.12), kind=kLoop, calls=%fused_computation.20 | loop fusion | flops 1331200 | bytes 2048000 | tf_op jit(solution)/shard_map/mul | solution.py:104
  3.1 3.1 %collective-permute-start.4 = (bf16[10,2048]{1,0:T(8,128)(2,1)S(1)}, bf16[10,2048]{1,0:T(8,128)(2,1)S(1)}, u32[]{:S(2)}, u32[]{:S(2)}) collective-permute-start(bf16[10,2048]{1,0:T(8,128)(2,1)S(1)} %bitcast.68), channel_id=1, source_target_pairs={{0,1},{1,2},{2,3},{3,4},{4,5},{5,6},{6,7},{7,8},{8,9},{9,10},{10,1... | collective-permute-start | bytes 122888 | tf_op jit(solution)/shard_map/ppermute | solution.py:117
  6.2 2.5 %collective-permute-start.12 = (bf16[10,2048]{1,0:T(8,128)(2,1)S(1)}, bf16[10,2048]{1,0:T(8,128)(2,1)S(1)}, u32[]{:S(2)}, u32[]{:S(2)}) collective-permute-start(bf16[10,2048]{1,0:T(8,128)(2,1)S(1)} %bitcast.69), channel_id=1, source_target_pairs={{1,0},{2,1},{3,2},{4,3},{5,4},{6,5},{7,6},{8,7},{9,8},{10,9},{11,1... | collective-permute-start | bytes 122888 | tf_op jit(solution)/shard_map/ppermute | solution.py:119
  8.8 1.4 %collective-permute-start.1 = (f32[2,50,1,128]{3,2,1,0:T(1,128)S(1)}, f32[2,50,1,128]{3,2,1,0:T(1,128)S(1)}, u32[]{:S(2)}, u32[]{:S(2)}) collective-permute-start(f32[2,50,1,128]{3,2,1,0:T(1,128)S(1)} %get-tuple-element.23), channel_id=1, source_target_pairs={{4,0},{8,4},{12,8},{16,12},{20,16},{24,20},{28,24},{5,1},{9,5},{13... | collective-permute-start | bytes 153608 | tf_op jit(solution)/shard_map/ppermute | solution.py:23
  10.2 3.0 %collective-permute-start = (f32[2,50,1,128]{3,2,1,0:T(1,128)S(1)}, f32[2,50,1,128]{3,2,1,0:T(1,128)S(1)}, u32[]{:S(2)}, u32[]{:S(2)}) collective-permute-start(f32[2,50,1,128]{3,2,1,0:T(1,128)S(1)} %get-tuple-element.22), channel_id=1, source_target_pairs={{0,4},{4,8},{8,12},{12,16},{16,20},{20,24},{24,28},{1,5},{5,9},{9,... | collective-permute-start | bytes 153608 | tf_op jit(solution)/shard_map/ppermute | solution.py:22
  14.0 4.9 %all-to-all-start.1 = ((s32[1,16,16]{2,0,1:T(1,128)}), s32[1,16,16]{2,0,1:T(1,128)S(1)}, u32[]{:S(2)}, u32[]{:S(2)}) async-start(s32[1,16,16]{2,0,1:T(1,128)} %all_to_all.14), calls=%async_computation.1 | async-start | bytes 16384 | tf_op jit(solution)/shard_map/all_to_all | solution.py:107
  18.9 0.9 fusion.22
  26.6 1.5 %collective-permute-start.5 = (bf16[10,2048]{1,0:T(8,128)(2,1)S(1)}, bf16[10,2048]{1,0:T(8,128)(2,1)}, u32[]{:S(2)}, u32[]{:S(2)}) collective-permute-start(bf16[10,2048]{1,0:T(8,128)(2,1)S(1)} %collective-permute-done.4), channel_id=1, source_target_pairs={{0,1},{1,2},{2,3},{3,4},{4,5},{5,6},{6,7},{7,8},{8,9},{9,10},{10,1... | collective-permute-start | bytes 122888 | tf_op jit(solution)/shard_map/ppermute | solution.py:117
  28.1 3.0 %collective-permute-start.13 = (bf16[10,2048]{1,0:T(8,128)(2,1)S(1)}, bf16[10,2048]{1,0:T(8,128)(2,1)}, u32[]{:S(2)}, u32[]{:S(2)}) collective-permute-start(bf16[10,2048]{1,0:T(8,128)(2,1)S(1)} %collective-permute-done.12), channel_id=1, source_target_pairs={{1,0},{2,1},{3,2},{4,3},{5,4},{6,5},{7,6},{8,7},{9,8},{10,9},{11,1... | collective-permute-start | bytes 122888 | tf_op jit(solution)/shard_map/ppermute | solution.py:119
  31.3 2.3 %collective-permute-done.5 = bf16[10,2048]{1,0:T(8,128)(2,1)} collective-permute-done((bf16[10,2048]{1,0:T(8,128)(2,1)S(1)}, bf16[10,2048]{1,0:T(8,128)(2,1)}, u32[]{:S(2)}, u32[]{:S(2)}) %collective-permute-start.5) | collective-permute-done | bytes 40992 | tf_op jit(solution)/shard_map/ppermute | solution.py:117
  34.1 1.0 copy.218
  35.1 1.3 %collective-permute-start.3 = (f32[2,50,18,1]{1,0,3,2:T(2,128)}, f32[2,50,18,1]{1,0,3,2:T(2,128)S(1)}, u32[]{:S(2)}, u32[]{:S(2)}) collective-permute-start(f32[2,50,18,1]{1,0,3,2:T(2,128)} %copy.218), channel_id=1, source_target_pairs={{1,0},{2,1},{3,2},{5,4},{6,5},{7,6},{9,8},{10,9},{11,10},{13,12},{... | collective-permute-start | bytes 21608 | tf_op jit(solution)/shard_map/ppermute | solution.py:23
  36.9 5.1 %collective-permute-start.2 = (f32[2,50,18,1]{1,0,3,2:T(2,128)S(1)}, f32[2,50,18,1]{1,0,3,2:T(2,128)}, u32[]{:S(2)}, u32[]{:S(2)}) collective-permute-start(f32[2,50,18,1]{1,0,3,2:T(2,128)S(1)} %copy.217), channel_id=1, source_target_pairs={{0,1},{1,2},{2,3},{4,5},{5,6},{6,7},{8,9},{9,10},{10,11},{12,13},{... | collective-permute-start | bytes 21608 | tf_op jit(solution)/shard_map/ppermute | solution.py:22
  43.2 1.3 %copy.219 = f32[2,50,18,1]{3,2,1,0:T(8,128)S(1)} copy(f32[2,50,18,1]{1,0,3,2:T(2,128)} %collective-permute-done.2) | data formatting | bytes 14400 | tf_op jit(solution)/shard_map/ppermute | solution.py:22
  44.5 4.5 %collective-permute-start.14 = (bf16[10,2048]{1,0:T(8,128)(2,1)}, bf16[10,2048]{1,0:T(8,128)(2,1)S(1)}, u32[]{:S(2)}, u32[]{:S(2)}) collective-permute-start(bf16[10,2048]{1,0:T(8,128)(2,1)} %collective-permute-done.13), channel_id=1, source_target_pairs={{1,0},{2,1},{3,2},{4,3},{5,4},{6,5},{7,6},{8,7},{9,8},{10,9},{11,1... | collective-permute-start | bytes 122888 | tf_op jit(solution)/shard_map/ppermute | solution.py:119
  49.0 1.5 %pad_maximum_fusion = f32[2,50,18,130]{3,2,1,0:T(8,128)S(1)} fusion(f32[2,50,18,1]{3,2,1,0:T(8,128)S(1)} %copy.220, f32[2,50,1,128]{3,2,1,0:T(1,128)S(1)} %collective-permute-done.1, f32[1,50,16,128]{3,2,1,0:T(8,128)S(1)} %bitcast.61, f32[1,50,16,128]{3,2,1,0:T(8,128)S(1)} %bitcast.64, f32[2,50,1,128]{3,2,1,0:T(1,128)S(1)} %collective-permute-done, ...), kind=kLoop, calls=%fused_computation.2 | loop fusion | flops 1170000 | bytes 1872000 | tf_op jit(solution)/shard_map/concatenate | solution.py:24
  51.2 4.4 %collective-permute-start.15 = (bf16[10,2048]{1,0:T(8,128)(2,1)S(1)}, bf16[10,2048]{1,0:T(8,128)(2,1)S(1)}, u32[]{:S(2)}, u32[]{:S(2)}) collective-permute-start(bf16[10,2048]{1,0:T(8,128)(2,1)S(1)} %collective-permute-done.14), channel_id=1, source_target_pairs={{1,0},{2,1},{3,2},{4,3},{5,4},{6,5},{7,6},{8,7},{9,8},{10,9},{11,1... | collective-permute-start | bytes 122888 | tf_op jit(solution)/shard_map/ppermute | solution.py:119
  55.9 1.6 %collective-permute-done.15 = bf16[10,2048]{1,0:T(8,128)(2,1)S(1)} collective-permute-done((bf16[10,2048]{1,0:T(8,128)(2,1)S(1)}, bf16[10,2048]{1,0:T(8,128)(2,1)S(1)}, u32[]{:S(2)}, u32[]{:S(2)}) %collective-permute-start.15) | collective-permute-done | bytes 40992 | tf_op jit(solution)/shard_map/ppermute | solution.py:119
  57.5 4.5 %collective-permute-start.16 = (bf16[10,2048]{1,0:T(8,128)(2,1)S(1)}, bf16[10,2048]{1,0:T(8,128)(2,1)S(1)}, u32[]{:S(2)}, u32[]{:S(2)}) collective-permute-start(bf16[10,2048]{1,0:T(8,128)(2,1)S(1)} %collective-permute-done.15), channel_id=1, source_target_pairs={{1,0},{2,1},{3,2},{4,3},{5,4},{6,5},{7,6},{8,7},{9,8},{10,9},{11,1... | collective-permute-start | bytes 122888 | tf_op jit(solution)/shard_map/ppermute | solution.py:119
  63.9 4.5 %collective-permute-start.17 = (bf16[10,2048]{1,0:T(8,128)(2,1)S(1)}, bf16[10,2048]{1,0:T(8,128)(2,1)S(1)}, u32[]{:S(2)}, u32[]{:S(2)}) collective-permute-start(bf16[10,2048]{1,0:T(8,128)(2,1)S(1)} %collective-permute-done.16), channel_id=1, source_target_pairs={{1,0},{2,1},{3,2},{4,3},{5,4},{6,5},{7,6},{8,7},{9,8},{10,9},{11,1... | collective-permute-start | bytes 122888 | tf_op jit(solution)/shard_map/ppermute | solution.py:119
  68.4 0.9 collective-permute-done.10
  70.3 4.6 %collective-permute-start.18 = (bf16[10,2048]{1,0:T(8,128)(2,1)S(1)}, bf16[10,2048]{1,0:T(8,128)(2,1)S(1)}, u32[]{:S(2)}, u32[]{:S(2)}) collective-permute-start(bf16[10,2048]{1,0:T(8,128)(2,1)S(1)} %collective-permute-done.17), channel_id=1, source_target_pairs={{1,0},{2,1},{3,2},{4,3},{5,4},{6,5},{7,6},{8,7},{9,8},{10,9},{11,1... | collective-permute-start | bytes 122888 | tf_op jit(solution)/shard_map/ppermute | solution.py:119
  74.9 0.9 collective-permute-done.11
  75.8 0.8 bitcast_dynamic-update-slice_fusion.10
  77.5 0.8 bitcast_dynamic-update-slice_fusion.8
  78.4 0.8 bitcast_dynamic-update-slice_fusion.5
  80.1 6.2 %copy.228 = bf16[10,16,2048]{0,2,1:T(8,128)(2,1)} copy(bf16[10,16,2048]{2,0,1:T(8,128)(2,1)S(1)} %bitcast.66) | data formatting | bytes 1310720 | tf_op jit(solution)/shard_map/reshape | solution.py:12
  86.2 5.4 %gather_fusion.1 = bf16[256,10]{1,0:T(8,128)(2,1)S(1)} fusion(bf16[10,32768]{0,1:T(8,128)(2,1)} %bitcast.65, s32[1024]{0:T(1024)} %pad_clamp_fusion), kind=kCustom, calls=%fused_computation.1 | custom fusion | bytes 11264 | tf_op jit(solution)/shard_map/jit(_take)/gather | solution.py:125
  94.0 1.3 %fusion.39 = (f32[10,256]{1,0:T(8,128)}, f32[10,256]{1,0:T(8,128)S(1)}) fusion(f32[10,256]{1,0:T(8,128)S(1)} %fusion.35, f32[9,256]{1,0:T(8,128)S(1)} %get-tuple-element.25, f32[1,256]{1,0:T(1,128)S(1)} %get-tuple-element.27, f32[1,256]{1,0:T(1,128)S(1)} %get-tuple-element.26, f32[9,256]{1,0:T(8,128)S(1)} %get-tuple-element.24, ...), kind=kLoop, calls=%fused_computation.85 | loop fusion | flops 43520 | bytes 59688 | tf_op jit(solution)/shard_map/sub | solution.py:136
  97.6 3.5 %all-to-all-start = ((bf16[10,16,16]{2,0,1:T(8,128)(2,1)}), bf16[10,16,16]{2,0,1:T(8,128)(2,1)S(1)}, u32[]{:S(2)}, u32[]{:S(2)}) async-start(bf16[10,16,16]{2,0,1:T(8,128)(2,1)} %pad_maximum_fusion.3), calls=%async_computation | async-start | bytes 131072 | tf_op jit(solution)/shard_map/all_to_all | solution.py:128
  101.1 1.6 %fusion.18 = f32[50,16,128]{2,1,0:T(8,128)S(1)} fusion(f32[50,16,128]{2,1,0:T(8,128)} %param.16, f32[50,16,128]{2,1,0:T(8,128)S(1)} %copy-done.2, f32[50,16,128]{2,1,0:T(8,128)S(1)} %copy-done.3, f32[50,16,129]{2,1,0:T(8,128)S(1)} %fusion.4, f32[50,17,128]{2,1,0:T(8,128)S(1)} %fusion.6, f32[1,16,128]{2,1,0:T(8,128)S(1)} %slice.218, ...), kind=kLoop, calls=%fused_computation.31 | loop fusion | flops 1945600 | bytes 4096000 | tf_op jit(solution)/shard_map/add | solution.py:140
  102.8 4.9 %all-to-all-done = bf16[10,16,16]{2,0,1:T(8,128)(2,1)S(1)} async-done(((bf16[10,16,16]{2,0,1:T(8,128)(2,1)}), bf16[10,16,16]{2,0,1:T(8,128)(2,1)S(1)}, u32[]{:S(2)}, u32[]{:S(2)}) %all-to-all-start) | async-done | bytes 5152 | tf_op jit(solution)/shard_map/all_to_all | solution.py:128
  (125 shorter events, 22.2 us)
Async XLA Ops:
  0.6 12.6 %copy-start.12 = (s32[256]{0:T(256)S(1)}, s32[256]{0:T(256)}, u32[]{:S(2)}) copy-start(s32[256]{0:T(256)} %param.19) | copy-start | bytes 3076
  0.7 12.6 %copy-start.13 = (s32[256]{0:T(256)S(1)}, s32[256]{0:T(256)}, u32[]{:S(2)}) copy-start(s32[256]{0:T(256)} %param.20) | copy-start | bytes 3076
  3.1 23.5 %collective-permute-start.4 = (bf16[10,2048]{1,0:T(8,128)(2,1)S(1)}, bf16[10,2048]{1,0:T(8,128)(2,1)S(1)}, u32[]{:S(2)}, u32[]{:S(2)}) collective-permute-start(bf16[10,2048]{1,0:T(8,128)(2,1)S(1)} %bitcast.68), channel_id=1, source_target_pairs={{0,1},{1,2},{2,3},{3,4},{4,5},{5,6},{6,7},{7,8},{8,9},{9,10},{10,1... | collective-permute-start | bytes 122888 | tf_op jit(solution)/shard_map/ppermute | solution.py:117
  6.2 21.9 %collective-permute-start.12 = (bf16[10,2048]{1,0:T(8,128)(2,1)S(1)}, bf16[10,2048]{1,0:T(8,128)(2,1)S(1)}, u32[]{:S(2)}, u32[]{:S(2)}) collective-permute-start(bf16[10,2048]{1,0:T(8,128)(2,1)S(1)} %bitcast.69), channel_id=1, source_target_pairs={{1,0},{2,1},{3,2},{4,3},{5,4},{6,5},{7,6},{8,7},{9,8},{10,9},{11,1... | collective-permute-start | bytes 122888 | tf_op jit(solution)/shard_map/ppermute | solution.py:119
  8.8 11.0 %copy-start.5 = (f32[10,256]{1,0:T(8,128)S(1)}, f32[10,256]{1,0:T(8,128)}, u32[]{:S(2)}) copy-start(f32[10,256]{1,0:T(8,128)} %param.18) | copy-start | bytes 30724
  8.8 14.0 %copy-start.16 = (f32[8]{0:T(128)S(1)}, f32[8]{0:T(128)}, u32[]{:S(2)}) copy-start(f32[8]{0:T(128)} %param.23) | copy-start | bytes 100
  8.8 15.4 %copy-start.9 = (s32[16,128]{1,0:T(8,128)S(1)}, s32[16,128]{1,0:T(8,128)}, u32[]{:S(2)}) copy-start(s32[16,128]{1,0:T(8,128)} %param.17) | copy-start | bytes 24580
  8.8 22.3 %collective-permute-start.1 = (f32[2,50,1,128]{3,2,1,0:T(1,128)S(1)}, f32[2,50,1,128]{3,2,1,0:T(1,128)S(1)}, u32[]{:S(2)}, u32[]{:S(2)}) collective-permute-start(f32[2,50,1,128]{3,2,1,0:T(1,128)S(1)} %get-tuple-element.23), channel_id=1, source_target_pairs={{4,0},{8,4},{12,8},{16,12},{20,16},{24,20},{28,24},{5,1},{9,5},{13... | collective-permute-start | bytes 153608 | tf_op jit(solution)/shard_map/ppermute | solution.py:23
  10.2 20.9 %collective-permute-start = (f32[2,50,1,128]{3,2,1,0:T(1,128)S(1)}, f32[2,50,1,128]{3,2,1,0:T(1,128)S(1)}, u32[]{:S(2)}, u32[]{:S(2)}) collective-permute-start(f32[2,50,1,128]{3,2,1,0:T(1,128)S(1)} %get-tuple-element.22), channel_id=1, source_target_pairs={{0,4},{4,8},{8,12},{12,16},{16,20},{20,24},{24,28},{1,5},{5,9},{9,... | collective-permute-start | bytes 153608 | tf_op jit(solution)/shard_map/ppermute | solution.py:22
  14.0 11.3 %all-to-all-start.1 = ((s32[1,16,16]{2,0,1:T(1,128)}), s32[1,16,16]{2,0,1:T(1,128)S(1)}, u32[]{:S(2)}, u32[]{:S(2)}) async-start(s32[1,16,16]{2,0,1:T(1,128)} %all_to_all.14), calls=%async_computation.1 | async-start | bytes 16384 | tf_op jit(solution)/shard_map/all_to_all | solution.py:107
  21.6 12.1 %copy-start.15 = (f32[10]{0:T(128)}, f32[10]{0:T(128)S(1)}, u32[]{:S(2)}) copy-start(f32[10]{0:T(128)S(1)} %add_negate_fusion) | copy-start | bytes 124
  22.9 10.8 %copy-start.11 = (f32[256]{0:T(256)}, f32[256]{0:T(256)S(1)}, u32[]{:S(2)}) copy-start(f32[256]{0:T(256)S(1)} %select_reduce_fusion) | copy-start | bytes 3076
  26.6 7.1 %collective-permute-start.5 = (bf16[10,2048]{1,0:T(8,128)(2,1)S(1)}, bf16[10,2048]{1,0:T(8,128)(2,1)}, u32[]{:S(2)}, u32[]{:S(2)}) collective-permute-start(bf16[10,2048]{1,0:T(8,128)(2,1)S(1)} %collective-permute-done.4), channel_id=1, source_target_pairs={{0,1},{1,2},{2,3},{3,4},{4,5},{5,6},{6,7},{7,8},{8,9},{9,10},{10,1... | collective-permute-start | bytes 122888 | tf_op jit(solution)/shard_map/ppermute | solution.py:117
  28.1 16.4 %collective-permute-start.13 = (bf16[10,2048]{1,0:T(8,128)(2,1)S(1)}, bf16[10,2048]{1,0:T(8,128)(2,1)}, u32[]{:S(2)}, u32[]{:S(2)}) collective-permute-start(bf16[10,2048]{1,0:T(8,128)(2,1)S(1)} %collective-permute-done.12), channel_id=1, source_target_pairs={{1,0},{2,1},{3,2},{4,3},{5,4},{6,5},{7,6},{8,7},{9,8},{10,9},{11,1... | collective-permute-start | bytes 122888 | tf_op jit(solution)/shard_map/ppermute | solution.py:119
  33.6 8.4 %collective-permute-start.6 = (bf16[10,2048]{1,0:T(8,128)(2,1)}, bf16[10,2048]{1,0:T(8,128)(2,1)}, u32[]{:S(2)}, u32[]{:S(2)}) collective-permute-start(bf16[10,2048]{1,0:T(8,128)(2,1)} %collective-permute-done.5), channel_id=1, source_target_pairs={{0,1},{1,2},{2,3},{3,4},{4,5},{5,6},{6,7},{7,8},{8,9},{9,10},{10,1... | collective-permute-start | bytes 122888 | tf_op jit(solution)/shard_map/ppermute | solution.py:117
  35.1 7.5 %collective-permute-start.3 = (f32[2,50,18,1]{1,0,3,2:T(2,128)}, f32[2,50,18,1]{1,0,3,2:T(2,128)S(1)}, u32[]{:S(2)}, u32[]{:S(2)}) collective-permute-start(f32[2,50,18,1]{1,0,3,2:T(2,128)} %copy.218), channel_id=1, source_target_pairs={{1,0},{2,1},{3,2},{5,4},{6,5},{7,6},{9,8},{10,9},{11,10},{13,12},{... | collective-permute-start | bytes 21608 | tf_op jit(solution)/shard_map/ppermute | solution.py:23
  36.9 6.3 %collective-permute-start.2 = (f32[2,50,18,1]{1,0,3,2:T(2,128)S(1)}, f32[2,50,18,1]{1,0,3,2:T(2,128)}, u32[]{:S(2)}, u32[]{:S(2)}) collective-permute-start(f32[2,50,18,1]{1,0,3,2:T(2,128)S(1)} %copy.217), channel_id=1, source_target_pairs={{0,1},{1,2},{2,3},{4,5},{5,6},{6,7},{8,9},{9,10},{10,11},{12,13},{... | collective-permute-start | bytes 21608 | tf_op jit(solution)/shard_map/ppermute | solution.py:22
  42.0 6.9 %collective-permute-start.7 = (bf16[10,2048]{1,0:T(8,128)(2,1)}, bf16[10,2048]{1,0:T(8,128)(2,1)}, u32[]{:S(2)}, u32[]{:S(2)}) collective-permute-start(bf16[10,2048]{1,0:T(8,128)(2,1)} %collective-permute-done.6), channel_id=1, source_target_pairs={{0,1},{1,2},{2,3},{3,4},{4,5},{5,6},{6,7},{7,8},{8,9},{9,10},{10,1... | collective-permute-start | bytes 122888 | tf_op jit(solution)/shard_map/ppermute | solution.py:117
  44.5 6.7 %collective-permute-start.14 = (bf16[10,2048]{1,0:T(8,128)(2,1)}, bf16[10,2048]{1,0:T(8,128)(2,1)S(1)}, u32[]{:S(2)}, u32[]{:S(2)}) collective-permute-start(bf16[10,2048]{1,0:T(8,128)(2,1)} %collective-permute-done.13), channel_id=1, source_target_pairs={{1,0},{2,1},{3,2},{4,3},{5,4},{6,5},{7,6},{8,7},{9,8},{10,9},{11,1... | collective-permute-start | bytes 122888 | tf_op jit(solution)/shard_map/ppermute | solution.py:119
  49.0 6.7 %collective-permute-start.8 = (bf16[10,2048]{1,0:T(8,128)(2,1)}, bf16[10,2048]{1,0:T(8,128)(2,1)S(1)}, u32[]{:S(2)}, u32[]{:S(2)}) collective-permute-start(bf16[10,2048]{1,0:T(8,128)(2,1)} %collective-permute-done.7), channel_id=1, source_target_pairs={{0,1},{1,2},{2,3},{3,4},{4,5},{5,6},{6,7},{7,8},{8,9},{9,10},{10,1... | collective-permute-start | bytes 122888 | tf_op jit(solution)/shard_map/ppermute | solution.py:117
  51.2 6.3 %collective-permute-start.15 = (bf16[10,2048]{1,0:T(8,128)(2,1)S(1)}, bf16[10,2048]{1,0:T(8,128)(2,1)S(1)}, u32[]{:S(2)}, u32[]{:S(2)}) collective-permute-start(bf16[10,2048]{1,0:T(8,128)(2,1)S(1)} %collective-permute-done.14), channel_id=1, source_target_pairs={{1,0},{2,1},{3,2},{4,3},{5,4},{6,5},{7,6},{8,7},{9,8},{10,9},{11,1... | collective-permute-start | bytes 122888 | tf_op jit(solution)/shard_map/ppermute | solution.py:119
  55.7 7.1 %collective-permute-start.9 = (bf16[10,2048]{1,0:T(8,128)(2,1)S(1)}, bf16[10,2048]{1,0:T(8,128)(2,1)S(1)}, u32[]{:S(2)}, u32[]{:S(2)}) collective-permute-start(bf16[10,2048]{1,0:T(8,128)(2,1)S(1)} %collective-permute-done.8), channel_id=1, source_target_pairs={{0,1},{1,2},{2,3},{3,4},{4,5},{5,6},{6,7},{7,8},{8,9},{9,10},{10,1... | collective-permute-start | bytes 122888 | tf_op jit(solution)/shard_map/ppermute | solution.py:117
  57.5 6.4 %collective-permute-start.16 = (bf16[10,2048]{1,0:T(8,128)(2,1)S(1)}, bf16[10,2048]{1,0:T(8,128)(2,1)S(1)}, u32[]{:S(2)}, u32[]{:S(2)}) collective-permute-start(bf16[10,2048]{1,0:T(8,128)(2,1)S(1)} %collective-permute-done.15), channel_id=1, source_target_pairs={{1,0},{2,1},{3,2},{4,3},{5,4},{6,5},{7,6},{8,7},{9,8},{10,9},{11,1... | collective-permute-start | bytes 122888 | tf_op jit(solution)/shard_map/ppermute | solution.py:119
  62.8 6.5 %collective-permute-start.10 = (bf16[10,2048]{1,0:T(8,128)(2,1)S(1)}, bf16[10,2048]{1,0:T(8,128)(2,1)S(1)}, u32[]{:S(2)}, u32[]{:S(2)}) collective-permute-start(bf16[10,2048]{1,0:T(8,128)(2,1)S(1)} %collective-permute-done.9), channel_id=1, source_target_pairs={{0,1},{1,2},{2,3},{3,4},{4,5},{5,6},{6,7},{7,8},{8,9},{9,10},{10,1... | collective-permute-start | bytes 122888 | tf_op jit(solution)/shard_map/ppermute | solution.py:117
  63.3 15.0 %copy-start.7 = (bf16[10,2048]{1,0:T(8,128)(2,1)S(1)}, bf16[10,2048]{1,0:T(8,128)(2,1)}, u32[]{:S(2)}) copy-start(bf16[10,2048]{1,0:T(8,128)(2,1)} %copy-done.6) | copy-start | bytes 122884
  63.9 6.4 %collective-permute-start.17 = (bf16[10,2048]{1,0:T(8,128)(2,1)S(1)}, bf16[10,2048]{1,0:T(8,128)(2,1)S(1)}, u32[]{:S(2)}, u32[]{:S(2)}) collective-permute-start(bf16[10,2048]{1,0:T(8,128)(2,1)S(1)} %collective-permute-done.16), channel_id=1, source_target_pairs={{1,0},{2,1},{3,2},{4,3},{5,4},{6,5},{7,6},{8,7},{9,8},{10,9},{11,1... | collective-permute-start | bytes 122888 | tf_op jit(solution)/shard_map/ppermute | solution.py:119
  69.3 6.5 %collective-permute-start.11 = (bf16[10,2048]{1,0:T(8,128)(2,1)S(1)}, bf16[10,2048]{1,0:T(8,128)(2,1)S(1)}, u32[]{:S(2)}, u32[]{:S(2)}) collective-permute-start(bf16[10,2048]{1,0:T(8,128)(2,1)S(1)} %collective-permute-done.10), channel_id=1, source_target_pairs={{0,1},{1,2},{2,3},{3,4},{4,5},{5,6},{6,7},{7,8},{8,9},{9,10},{10,1... | collective-permute-start | bytes 122888 | tf_op jit(solution)/shard_map/ppermute | solution.py:117
  70.3 9.0 %collective-permute-start.18 = (bf16[10,2048]{1,0:T(8,128)(2,1)S(1)}, bf16[10,2048]{1,0:T(8,128)(2,1)S(1)}, u32[]{:S(2)}, u32[]{:S(2)}) collective-permute-start(bf16[10,2048]{1,0:T(8,128)(2,1)S(1)} %collective-permute-done.17), channel_id=1, source_target_pairs={{1,0},{2,1},{3,2},{4,3},{5,4},{6,5},{7,6},{8,7},{9,8},{10,9},{11,1... | collective-permute-start | bytes 122888 | tf_op jit(solution)/shard_map/ppermute | solution.py:119
  80.1 21.0 %copy-start.4 = (f32[49,16,128]{2,1,0:T(8,128)S(1)}, f32[49,16,128]{2,1,0:T(8,128)}, u32[]{:S(2)}) copy-start(f32[49,16,128]{2,1,0:T(8,128)} %fusion.22) | copy-start | bytes 1204228
  86.2 14.8 %copy-start.2 = (f32[50,16,128]{2,1,0:T(8,128)S(1)}, f32[50,16,128]{2,1,0:T(8,128)}, u32[]{:S(2)}) copy-start(f32[50,16,128]{2,1,0:T(8,128)} %copy-done.1) | copy-start | bytes 1228804
  86.2 14.8 %copy-start.3 = (f32[50,16,128]{2,1,0:T(8,128)S(1)}, f32[50,16,128]{2,1,0:T(8,128)}, u32[]{:S(2)}) copy-start(f32[50,16,128]{2,1,0:T(8,128)} %param.15) | copy-start | bytes 1228804
  97.6 10.1 %all-to-all-start = ((bf16[10,16,16]{2,0,1:T(8,128)(2,1)}), bf16[10,16,16]{2,0,1:T(8,128)(2,1)S(1)}, u32[]{:S(2)}, u32[]{:S(2)}) async-start(bf16[10,16,16]{2,0,1:T(8,128)(2,1)} %pad_maximum_fusion.3), calls=%async_computation | async-start | bytes 131072 | tf_op jit(solution)/shard_map/all_to_all | solution.py:128
  (6 other events, 34.8 us)
